TPU v7x, 32 devices: a whole 2x2x4 slice. The times are simulated.
32 devices in a mesh: tm: 2 (over y), obs: 16 (over z, x, core).
Axes of the slice: x: 2, y: 2, z: 4, core: 2. Of those that a mesh axis runs over, the one named last changes fastest.
Arguments:
- flux: bfloat16 [4, 64, 16384], P('tm', 'obs'), may hold values from -6 to 6
- footprint: bfloat16 [2048, 16384], P(('tm', 'obs')), may hold values from -0.046875 to 0.046875
- entry_owner: int32 [2048, 1], P(('tm', 'obs')), may hold values from 0 to 15; in each aligned block of 64 rows (0 to 63, 64 to 127, ...) at most 8 rows name the same one
- entry_tile: int32 [32, 64], P(('tm', 'obs')), may hold values from 0 to 3
- entry_lag: int32 [32, 64], P(('tm', 'obs')), may hold values from 0 to 1
- entry_sounding: int32 [32, 64], P(('tm', 'obs')), may hold values from 0 to 15, never falling along the last dimension, each value on 1 to 8 neighbouring positions
- sounding_window: int32 [32, 16], P(('tm', 'obs')), may hold values from 1 to 3
- observed: float32 [32, 16], P(('tm', 'obs')), may hold values from -8 to 8
- obs_weight: float32 [32, 16], P(('tm', 'obs')), may hold values from 0.25 to 4
Outputs:
- modeled: float32 [32, 16], P(('tm', 'obs'))
- gradient: float32 [4, 64, 16384], P('tm', 'obs')
Inputs may be any that keep to these rules, and one draw needn't show every extreme that they name: `entry_owner`: among the 64 entries of one device no owner is named more than 8 times, and on some device some owner is named exactly 8 times.
All inputs are finite; a program needn't handle non-finite values.
Results may differ from a plain program's by a relative error of at most 0.0029.
Values may be sent and summed in bfloat16 or wider, within the bound.
A program may use at most 64 MiB of HBM per device.

v0:
```python
import functools

import jax
import jax.numpy as jnp
from jax import lax
from jax.experimental import pallas as pl
from jax.experimental.pallas import tpu as pltpu
from jax.sharding import PartitionSpec as P


def per_device(
    flux,
    footprint,
    entry_owner,
    entry_tile,
    entry_lag,
    entry_sounding,
    sounding_window,
    observed,
    obs_weight,
):
    peer_count = lax.axis_size("obs")
    entry_count = footprint.shape[0]
    cell_count = footprint.shape[1]
    tile_dev = flux.shape[1]
    sounding_count = observed.shape[1]
    slot_cap = 2 * entry_count // peer_count
    owners = entry_owner[:, 0]
    sounding = entry_sounding[0]
    sounding_hot = sounding[:, None] == jnp.arange(sounding_count, dtype=jnp.int32)[None, :]
    window = jnp.sum(jnp.where(sounding_hot, sounding_window[0][None, :], 0), axis=1) - entry_lag[0]
    target = window * tile_dev + entry_tile[0]
    owner_hot = (owners[:, None] == jnp.arange(peer_count, dtype=jnp.int32)[None, :]).astype(
        jnp.int32
    )
    rank_within = jnp.sum((jnp.cumsum(owner_hot, axis=0) - owner_hot) * owner_hot, axis=1)
    slot_index = owners * slot_cap + rank_within
    send_blocks = (
        jnp.zeros((peer_count * slot_cap, cell_count), jnp.bfloat16).at[slot_index].set(footprint)
    )
    send_blocks = send_blocks.reshape(peer_count, slot_cap, cell_count)
    send_target = jnp.zeros((peer_count * slot_cap,), jnp.int32).at[slot_index].set(target)
    send_target = send_target.reshape(peer_count, slot_cap)
    everything = lax.all_gather(flux, "tm", axis=0, tiled=True).reshape(-1, cell_count)
    got_blocks, got_target = (
        lax.all_to_all(send_blocks, "obs", split_axis=0, concat_axis=0, tiled=True),
        lax.all_to_all(send_target, "obs", split_axis=0, concat_axis=0, tiled=True),
    )
    selected = everything[got_target.reshape(-1)].reshape(got_blocks.shape)
    returned = lax.all_to_all(
        jnp.einsum("pkc,pkc->pk", got_blocks, selected, preferred_element_type=jnp.float32),
        "obs",
        split_axis=0,
        concat_axis=0,
        tiled=True,
    )
    entry_dots = returned.reshape(-1)[slot_index]
    modeled = jnp.sum(jnp.where(sounding_hot, entry_dots[:, None], 0.0), axis=0)
    residual = obs_weight[0] * (modeled - observed[0])
    entry_resid = jnp.sum(jnp.where(sounding_hot, residual[None, :], 0.0), axis=1)
    slot_resid = jnp.zeros((peer_count * slot_cap,), jnp.float32).at[slot_index].set(entry_resid)
    got_resid = lax.all_to_all(
        slot_resid.reshape(peer_count, slot_cap), "obs", split_axis=0, concat_axis=0, tiled=True
    )
    contribution = (got_resid[:, :, None] * got_blocks).astype(jnp.bfloat16)
    targets = got_target
    contribution = contribution.reshape(-1, cell_count)
    targets = targets.reshape(-1)
    row_count = flux.shape[0] * lax.axis_size("tm")
    row_ids = jnp.arange(row_count * tile_dev, dtype=jnp.int32)
    row_match = (row_ids[:, None] == targets[None, :]).astype(jnp.bfloat16)
    summed = jnp.dot(row_match, contribution, preferred_element_type=jnp.float32)
    gradient = lax.psum_scatter(
        summed.reshape(row_count, tile_dev * cell_count), "tm", scatter_dimension=0, tiled=True
    )
    gradient = gradient.reshape(flux.shape[0], tile_dev, cell_count)
    return (modeled[None, :], gradient)


KINDS = (
    "foot", "flux", "m0", "m1", "m2", "m3", "m4", "m5", "m6", "vals",
    "gup0", "gup1", "gup2", "gdown0", "gdown1", "gdown2", "g1x", "g1y", "g2x", "g2y",
    "s1x", "s1y", "s2x", "s2y", "z0", "z1", "fin",
)
KIND = {name: at for at, name in enumerate(KINDS)}


def eye(n):
    return lax.broadcasted_iota(jnp.int32, (n, n), 0) == lax.broadcasted_iota(jnp.int32, (n, n), 1)


def to_col(row):
    return jnp.sum(jnp.where(eye(row.shape[1]), row, 0.0), axis=1, keepdims=True)


def to_row(col):
    return jnp.sum(jnp.where(eye(col.shape[0]), col, 0.0), axis=0, keepdims=True)


def chip_kernel(
    depth, windows, tile_dev, flux, foot, owner, tile, lag, sounding, swin, observed, weight,
    modeled_out, out,
    foot_all, contrib, gath, owner_p, tile_p, lag_p, sounding_p, swin_p, observed_p, weight_p,
    val_send, val_recv, row_ids, staged, t1x, t1y, a1x, a1y, t2x, t2y, a2x, a2y, keep_x, keep_y, tz, az, zsum,
    send_sem, recv_sem, local_sem,
):
    entries = foot.shape[0]
    half = foot.shape[1] // 2
    quarter = half // 2
    rows_dev = windows * tile_dev
    rows_chip = 2 * rows_dev
    rows_plane = 4 * rows_chip
    extra = quarter // 2048 * 384
    tile_cells = min(1024, quarter)
    tile_back = min(1024, quarter)
    y = lax.axis_index("tm")
    o = lax.axis_index("obs")
    core = lax.rem(o, 2)
    x = lax.rem(o // 2, 2)
    z = o // 4
    partner = (y, o + 1 - 2 * core)
    xn = (y, o + 2 - 4 * x)
    yn = (1 - y, o)
    zu = (y, o + 4)
    zd = (y, o - 4)
    has_up = z < depth - 1
    has_down = z > 0

    def nearest(k):
        picked = z
        for place in range(depth):
            order = sorted(range(depth), key=lambda other_z: (abs(other_z - place), other_z))
            picked = jnp.where(z == place, order[k], picked)
        return picked

    def along_z(zz):
        return (y, o + 4 * (zz - z))

    mine = pl.ds(pl.multiple_of(core * half, half), half)
    other = pl.ds(pl.multiple_of((1 - core) * half, half), half)
    low, high = pl.ds(0, quarter), pl.ds(quarter, quarter)
    local_flux = pltpu.make_async_copy(flux.at[:, :, mine], staged.at[0], local_sem.at[0])
    local_foot = pltpu.make_async_copy(foot.at[:, mine], foot_all.at[0], local_sem.at[1])
    barrier = pltpu.get_barrier_semaphore()
    for device in (partner, xn, yn, *(along_z(nearest(k)) for k in range(1, depth))):
        pl.semaphore_signal(
            barrier, inc=1, device_id=device, device_id_type=pl.DeviceIdType.MESH
        )
    local_flux.start()
    local_foot.start()
    pl.semaphore_wait(barrier, 2 + depth)

    def remote(kind, at, src, dst, device):
        return pltpu.make_async_remote_copy(
            src_ref=src,
            dst_ref=dst,
            send_sem=send_sem.at[KIND[kind], at],
            recv_sem=recv_sem.at[KIND[kind], at],
            device_id=device,
            device_id_type=pl.DeviceIdType.MESH,
        )

    fixed = [
        remote("flux", 0, flux.at[:, :, other], staged.at[1], partner),
        remote("foot", 0, foot.at[:, other], foot_all.at[1], partner),
    ]
    pairs = (
        (owner, owner_p), (tile, tile_p), (lag, lag_p), (sounding, sounding_p),
        (swin, swin_p), (observed, observed_p), (weight, weight_p),
    )
    for at, (src, dst) in enumerate(pairs):
        fixed.append(remote(f"m{at}", 0, src, dst, partner))
    for copy in fixed:
        copy.start()

    def gather_z(zz, part, upward):
        cells = (
            pl.ds(0, quarter - extra),
            pl.ds(quarter + extra, quarter - extra),
            pl.ds(quarter - extra, 2 * extra),
        )[part]
        block = gath.at[zz, :, :, :, cells] if part == 2 else gath.at[zz, y, x, :, cells]
        kind = ("gup" if upward else "gdown") + str(part)
        return remote(kind, zz, block, block, zu if upward else zd)

    def send_z(zz, parts):
        for part in parts:
            pl.when((zz <= z) & has_up)(lambda: gather_z(zz, part, True).start())
            pl.when((zz >= z) & has_down)(lambda: gather_z(zz, part, False).start())

    def take_z(zz, parts):
        for part in parts:
            pl.when(zz < z)(lambda: gather_z(zz, part, True).wait_recv())
            pl.when(zz > z)(lambda: gather_z(zz, part, False).wait_recv())

    def low_of(own):
        return low if own else pl.ds(0, quarter - extra)

    def high_of(own):
        return high if own else pl.ds(quarter + extra, quarter - extra)

    def gather_1x(zz, own):
        block = gath.at[zz, y, x, :, low_of(own)]
        return remote("g1x", zz, block, block, xn)

    def gather_1y(zz, own):
        block = gath.at[zz, y, x, :, high_of(own)]
        return remote("g1y", zz, block, block, yn)

    def gather_2x(zz, own):
        block = gath.at[zz, :, x, :, high_of(own)]
        return remote("g2x", zz, block, block, xn)

    def gather_2y(zz, own):
        block = gath.at[zz, y, :, :, low_of(own)]
        return remote("g2y", zz, block, block, yn)

    def fields(refs):
        owner_r, tile_r, lag_r, sounding_r, swin_r, _, _ = refs
        count = swin_r.shape[1]
        hot = lax.broadcasted_iota(jnp.int32, (count, entries), 0) == sounding_r[...]
        window = jnp.sum(
            jnp.where(hot, to_col(swin_r[...].astype(jnp.float32)), 0.0), axis=0, keepdims=True
        ) - lag_r[...].astype(jnp.float32)
        window = window.astype(jnp.int32)
        own = owner_r[...]
        late = jnp.where(window >= windows, 1, 0)
        chip = ((own >> 2) * 2 + late) * 2 + ((own >> 1) & 1)
        inner = (own & 1) * rows_dev + (window - late * windows) * tile_dev + tile_r[...]
        return hot, chip * rows_chip + inner

    sets = (
        (owner, tile, lag, sounding, swin, observed, weight),
        (owner_p, tile_p, lag_p, sounding_p, swin_p, observed_p, weight_p),
    )
    hots, ids = [None, None], [None, None]
    hots[0], ids[0] = fields(sets[0])

    local_flux.wait()
    fixed[0].wait_recv()

    def place(step, carry):
        cells = pl.ds(pl.multiple_of(step * tile_cells, tile_cells), tile_cells)
        own_rows = staged[0, :, :, cells].reshape(rows_dev, tile_cells)
        other_rows = staged[1, :, :, cells].reshape(rows_dev, tile_cells)
        gath[z, y, x, :, cells] = jnp.concatenate(
            [jnp.where(core == 0, own_rows, other_rows), jnp.where(core == 0, other_rows, own_rows)],
            axis=0,
        )
        return carry

    lax.fori_loop(0, half // tile_cells, place, 0)
    def arrive(k):
        zz = nearest(k)
        if k > 0:
            take_z(zz, (0, 1))
        send_z(zz, (0, 1))
        gather_1x(zz, k == 0).start()
        gather_1y(zz, k == 0).start()

    def widen(k):
        zz = nearest(k)
        gather_1x(zz, k == 0).wait_recv()
        gather_1y(zz, k == 0).wait_recv()
        gather_2x(zz, k == 0).start()
        gather_2y(zz, k == 0).start()

    def complete(k):
        zz = nearest(k)
        gather_2x(zz, k == 0).wait_recv()
        gather_2y(zz, k == 0).wait_recv()

    def spread(k):
        zz = nearest(k)
        if k > 0:
            take_z(zz, (2,))
        send_z(zz, (2,))

    def values(k, total, ids_col):
        zz = nearest(k)

        def dots(step, acc):
            cells = pl.ds(pl.multiple_of(step * quarter, quarter), quarter)
            return acc + lax.dot_general(
                foot_all[:, :, cells].reshape(2 * entries, quarter),
                gath[zz, :, :, :, cells].reshape(rows_plane, quarter),
                (((1,), (1,)), ((), ())),
                preferred_element_type=jnp.float32,
            )

        acc = lax.fori_loop(
            0, half // quarter, dots, jnp.zeros((2 * entries, rows_plane), jnp.float32)
        )
        lanes = lax.broadcasted_iota(jnp.int32, (2 * entries, rows_plane), 1) + zz * rows_plane
        return total + jnp.sum(jnp.where(ids_col == lanes, acc, 0.0), axis=1, keepdims=True)

    arrive(0)
    widen(0)
    total = jnp.zeros((2 * entries, 1), jnp.float32)
    arrive(1)
    complete(0)
    spread(0)
    for copy in fixed[1:]:
        copy.wait_recv()
    local_foot.wait()
    hots[1], ids[1] = fields(sets[1])
    row_ids[...] = jnp.concatenate(ids, axis=1)
    ids_col = jnp.concatenate(
        [to_col(i.astype(jnp.float32)).astype(jnp.int32) for i in ids], axis=0
    )
    total = values(0, total, ids_col)
    for k in range(2, depth):
        arrive(k)
        if k < depth - 1:
            widen(k - 1)
    widen(max(depth - 2, 1))
    if depth > 2:
        widen(depth - 1)
    spread(1)
    if depth > 2:
        spread(2)
    for k in range(1, depth):
        complete(k)
        if k > 2:
            spread(k)
        total = values(k, total, ids_col)

    for h in range(2):
        val_send[h] = to_row(total[h * entries : (h + 1) * entries])
    vals = remote("vals", 0, val_send, val_recv, partner)
    vals.start()
    vals.wait_recv()
    resids = []
    for h in range(2):
        value = val_send[h] + val_recv[1 - h]
        modeled = to_row(jnp.sum(jnp.where(hots[h], value, 0.0), axis=1, keepdims=True))
        if h == 0:
            modeled_out[...] = modeled
        residual = sets[h][6][...] * (modeled - sets[h][5][...])
        resids.append(
            to_col(jnp.sum(jnp.where(hots[h], to_col(residual), 0.0), axis=0, keepdims=True))
        )

    def over(offset, body):
        def step_body(step, carry):
            at = pl.multiple_of(step * tile_back, tile_back)
            body(pl.ds(at, tile_back), pl.ds(offset + at, tile_back))
            return carry

        lax.fori_loop(0, quarter // tile_back, step_body, 0)

    def scale(near, cells):
        for h in range(2):
            scaled = resids[h] * foot_all[h, :, cells].astype(jnp.float32)
            contrib[pl.ds(h * entries, entries), cells] = scaled.astype(jnp.bfloat16)

    def pick_rows(*bases):
        own = lax.broadcasted_iota(jnp.int32, (rows_chip, 2 * entries), 0)
        rows = jnp.concatenate([own + base for base in bases], axis=0)
        return jnp.where(row_ids[...] == rows, 1.0, 0.0).astype(jnp.bfloat16)

    def scatter_1x(zz):
        return remote("s1x", zz, t1x.at[zz], a1x.at[zz], xn)

    def scatter_1y(zz):
        return remote("s1y", zz, t1y.at[zz], a1y.at[zz], yn)

    def scatter_2x(zz):
        return remote("s2x", zz, t2x.at[zz], a2x.at[zz], xn)

    def scatter_2y(zz):
        return remote("s2y", zz, t2y.at[zz], a2y.at[zz], yn)

    def scatter_z(zz, part):
        cells = high if part else low
        kind = KIND[f"z{part}"]
        return pltpu.make_async_remote_copy(
            src_ref=tz.at[zz, :, cells],
            dst_ref=az.at[z, :, cells],
            send_sem=send_sem.at[kind, zz],
            recv_sem=recv_sem.at[kind, z],
            device_id=along_z(zz),
            device_id_type=pl.DeviceIdType.MESH,
        )

    def from_z(zz, part):
        cells = high if part else low
        kind = KIND[f"z{part}"]
        return pltpu.make_async_remote_copy(
            src_ref=tz.at[zz, :, cells],
            dst_ref=az.at[zz, :, cells],
            send_sem=send_sem.at[kind, zz],
            recv_sem=recv_sem.at[kind, zz],
            device_id=along_z(zz),
            device_id_type=pl.DeviceIdType.MESH,
        )

    def finish(part, far):
        cells = high if part else low
        into = pl.ds(pl.multiple_of(core * half + part * quarter, quarter), quarter)
        if far:
            return remote("fin", part, zsum.at[1 - core, :, cells], out.at[:, into], partner)
        return pltpu.make_async_copy(zsum.at[core, :, cells], out.at[:, into], local_sem.at[part])

    def first(zz, fresh):
        def chip(yy, xx):
            return ((zz * 2 + yy) * 2 + xx) * rows_chip

        def run(offset, bases, sent, kept):
            pick = pick_rows(*bases)

            def body(near, cells):
                summed = jnp.dot(pick, contrib[:, cells], preferred_element_type=jnp.float32)
                summed = summed.reshape(2, 2, rows_chip, tile_back)
                sent[zz, :, :, near] = summed[0].astype(jnp.bfloat16)
                kept[zz, :, :, near] = summed[1]

            if fresh:
                over(offset, scale)
            over(offset, body)

        run(0, (chip(0, 1 - x), chip(1, 1 - x), chip(0, x), chip(1, x)), t1x, keep_x)
        scatter_1x(zz).start()
        run(quarter, (chip(1 - y, 0), chip(1 - y, 1), chip(y, 0), chip(y, 1)), t1y, keep_y)
        scatter_1y(zz).start()

    def second(zz):
        def for_y(near, cells):
            got = a1x[zz, 1 - y, :, near].astype(jnp.float32)
            t2y[zz, :, near] = (keep_x[zz, 1 - y, :, near] + got).astype(jnp.bfloat16)

        def for_x(near, cells):
            got = a1y[zz, 1 - x, :, near].astype(jnp.float32)
            t2x[zz, :, near] = (keep_y[zz, 1 - x, :, near] + got).astype(jnp.bfloat16)

        scatter_1x(zz).wait_recv()
        over(0, for_y)
        scatter_2y(zz).start()
        scatter_1y(zz).wait_recv()
        over(quarter, for_x)
        scatter_2x(zz).start()

    def third(zz, part, last):
        def plane_sum(near):
            if part:
                return keep_y[zz, x, :, near] + (
                    a1y[zz, x, :, near].astype(jnp.float32) + a2x[zz, :, near].astype(jnp.float32)
                )
            return keep_x[zz, y, :, near] + (
                a1x[zz, y, :, near].astype(jnp.float32) + a2y[zz, :, near].astype(jnp.float32)
            )

        def send_on(near, cells):
            tz[zz, :, cells] = plane_sum(near).astype(jnp.bfloat16)

        def sum_up(near, cells):
            summed = plane_sum(near)
            for k in range(1, depth):
                summed = summed + az[nearest(k), :, cells].astype(jnp.float32)
            zsum[:, :, cells] = summed.reshape(2, rows_dev, tile_back)

        (scatter_2x if part else scatter_2y)(zz).wait_recv()
        if last:
            for k in range(1, depth):
                from_z(nearest(k), part).wait_recv()
            over(part * quarter, sum_up)
        else:
            over(part * quarter, send_on)
            scatter_z(zz, part).start()

    def leave(k):
        for part in range(2):
            third(nearest(depth - 1 - k), part, k == depth - 1)
            if k == depth - 1:
                finish(part, True).start()
                finish(part, False).start()

    for k in range(depth - 1):
        first(nearest(depth - 1 - k), k == 0)
        if k > 0:
            second(nearest(depth - k))
        if k > 1:
            leave(k - 2)
    second(nearest(1))
    first(nearest(0), False)
    for k in range(max(depth - 3, 0), depth - 1):
        leave(k)
    second(nearest(0))
    leave(depth - 1)
    for part in range(2):
        finish(part, False).wait()
        finish(part, True).wait()
    for copy in fixed:
        copy.wait_send()
    vals.wait_send()
    for k in range(1, depth):
        for part in range(2):
            scatter_z(nearest(k), part).wait_send()

    def drain(zz, carry):
        for part in range(3):
            pl.when((zz <= z) & has_up)(lambda: gather_z(zz, part, True).wait_send())
            pl.when((zz >= z) & has_down)(lambda: gather_z(zz, part, False).wait_send())
        for copy in (scatter_1x, scatter_1y, scatter_2x, scatter_2y):
            copy(zz).wait_send()
        return carry

    lax.fori_loop(0, depth, drain, 0)
    for k in range(depth):
        for copy in (gather_1x, gather_1y, gather_2x, gather_2y):
            copy(nearest(k), k == 0).wait_send()


def per_chip(depth, flux, footprint, owner, tile, lag, sounding, swin, observed, weight):
    windows, tile_dev, cells = flux.shape
    entries = footprint.shape[0]
    rows_dev = windows * tile_dev
    rows_chip = 2 * rows_dev
    half, quarter = cells // 2, cells // 4
    sounds = observed.shape[1]
    bf, f32, i32 = jnp.bfloat16, jnp.float32, jnp.int32
    vmem, hbm = pl.BlockSpec(memory_space=pltpu.VMEM), pl.BlockSpec(memory_space=pl.ANY)
    modeled, gradient = pl.pallas_call(
        functools.partial(chip_kernel, depth, windows, tile_dev),
        out_shape=(
            jax.ShapeDtypeStruct((1, sounds), f32),
            jax.ShapeDtypeStruct((rows_dev, cells), f32),
        ),
        in_specs=[hbm, hbm] + [vmem] * 7,
        out_specs=(vmem, vmem),
        scratch_shapes=[
            pltpu.VMEM((2, entries, half), bf),
            pltpu.VMEM((2 * entries, half), bf),
            pltpu.VMEM((depth, 2, 2, rows_chip, half), bf),
            pltpu.VMEM((1, entries), i32),
            pltpu.VMEM((1, entries), i32),
            pltpu.VMEM((1, entries), i32),
            pltpu.VMEM((1, entries), i32),
            pltpu.VMEM((1, sounds), i32),
            pltpu.VMEM((1, sounds), f32),
            pltpu.VMEM((1, sounds), f32),
            pltpu.VMEM((2, 1, entries), f32),
            pltpu.VMEM((2, 1, entries), f32),
            pltpu.VMEM((1, 2 * entries), i32),
            pltpu.VMEM((2, windows, tile_dev, half), bf),
            *[pltpu.VMEM((depth, 2, rows_chip, quarter), bf)] * 4,
            *[pltpu.VMEM((depth, rows_chip, quarter), bf)] * 4,
            *[pltpu.VMEM((depth, 2, rows_chip, quarter), f32)] * 2,
            *[pltpu.VMEM((depth, rows_chip, half), bf)] * 2,
            pltpu.VMEM((2, rows_dev, half), f32),
            pltpu.SemaphoreType.DMA((len(KINDS), depth)),
            pltpu.SemaphoreType.DMA((len(KINDS), depth)),
            pltpu.SemaphoreType.DMA((2,)),
        ],
        compiler_params=pltpu.CompilerParams(collective_id=0, has_side_effects=True),
    )(flux, footprint, owner.reshape(1, entries), tile, lag, sounding, swin, observed, weight)
    return modeled, gradient.reshape(windows, tile_dev, cells)


def solution(mesh):
    placed = (
        P("tm", "obs", None),
        P(("tm", "obs"), None),
        P(("tm", "obs"), None),
        P(("tm", "obs"), None),
        P(("tm", "obs"), None),
        P(("tm", "obs"), None),
        P(("tm", "obs"), None),
        P(("tm", "obs"), None),
        P(("tm", "obs"), None),
    )
    times, places = mesh.shape["tm"], mesh.shape["obs"]
    depth = places // 4
    grouped = times == 2 and places % 4 == 0 and depth >= 2

    def routed(flux, *rest):
        rows = flux.shape[0] * flux.shape[1] * times * places
        fits = rows * flux.shape[2] * 8 <= 40 * 2**20
        plain = flux.shape[0] * flux.shape[1] % 8 == 0 and flux.shape[2] % 8192 == 0
        body = functools.partial(per_chip, depth) if grouped and fits and plain else per_device
        return body(flux, *rest)

    return jax.shard_map(
        routed,
        mesh=mesh,
        in_specs=placed,
        out_specs=(P(("tm", "obs"), None), P("tm", "obs", None)),
        check_vma=False,
    )
```

profile of v0, /device:TPU:0, one launch (start us, length us, event | category | flops | bytes accessed | tf_op | source)
XLA Modules:
  0.0 98.0 jit_solution(480612282501098403)
XLA Ops:
  0.6 94.2 %shard_map.104 = (f32[1,16]{1,0:T(1,128)}, f32[8,16384]{1,0:T(8,128)}) custom-call(bf16[2,4,16384]{2,1,0:T(4,128)(2,1)} %flux.1, bf16[64,16384]{1,0:T(8,128)(2,1)} %foot.1, s32[1,64]{1,0:T(1,128)} %bitcast.1, s32[1,64]{1,0:T(1,128)} %tile.1, s32[1,64]{1,0:T(1,128)} %lag.1, s32[1,64]{1,0:T(1,128)} %sounding.1, s32[1,16]{1,0:T(1,128)} %swin.1, ...), custom_call_target="tpu_custom_call" | custom-call | tf_op jit(solution)/shard_map/pallas_call | solution.py:523
  94.9 2.0 %reshape.11 = f32[2,4,16384]{2,1,0:T(4,128)} reshape(f32[8,16384]{1,0:T(8,128)} %get-tuple-element.5) | data formatting | bytes 1048576 | tf_op jit(solution)/shard_map/reshape | solution.py:557
  96.9 1.1 %copy.12 = f32[1,16]{1,0:T(1,128)} copy(f32[1,16]{1,0:T(1,128)} %get-tuple-element.8) | data formatting | bytes 128
where the time goes:
time: 98.1 us; the launch traced here: 98 us
  Pallas kernels  94.2 us (96%)
  local copies, waits for them, and re-layouts  3.09 us (3%)
    pallas_call x1, Pallas kernels, per_chip(): pl.pallas_call(functools.partial(chip_kernel, depth, windows, tile_dev),...  94.2 us
    reshape x1, local copies, waits for them, and re-layouts, per_chip(): return (modeled, gradient.reshape(windows, tile_dev, cells))  1.98 us

commit v1 on v0

v1 whole, which is shorter than its diff:
```python
import functools

import jax
import jax.numpy as jnp
from jax import lax
from jax.experimental import pallas as pl
from jax.experimental.pallas import tpu as pltpu
from jax.sharding import PartitionSpec as P


def per_device(
    flux,
    footprint,
    entry_owner,
    entry_tile,
    entry_lag,
    entry_sounding,
    sounding_window,
    observed,
    obs_weight,
):
    peer_count = lax.axis_size("obs")
    entry_count = footprint.shape[0]
    cell_count = footprint.shape[1]
    tile_dev = flux.shape[1]
    sounding_count = observed.shape[1]
    slot_cap = 2 * entry_count // peer_count
    owners = entry_owner[:, 0]
    sounding = entry_sounding[0]
    sounding_hot = sounding[:, None] == jnp.arange(sounding_count, dtype=jnp.int32)[None, :]
    window = jnp.sum(jnp.where(sounding_hot, sounding_window[0][None, :], 0), axis=1) - entry_lag[0]
    target = window * tile_dev + entry_tile[0]
    owner_hot = (owners[:, None] == jnp.arange(peer_count, dtype=jnp.int32)[None, :]).astype(
        jnp.int32
    )
    rank_within = jnp.sum((jnp.cumsum(owner_hot, axis=0) - owner_hot) * owner_hot, axis=1)
    slot_index = owners * slot_cap + rank_within
    send_blocks = (
        jnp.zeros((peer_count * slot_cap, cell_count), jnp.bfloat16).at[slot_index].set(footprint)
    )
    send_blocks = send_blocks.reshape(peer_count, slot_cap, cell_count)
    send_target = jnp.zeros((peer_count * slot_cap,), jnp.int32).at[slot_index].set(target)
    send_target = send_target.reshape(peer_count, slot_cap)
    everything = lax.all_gather(flux, "tm", axis=0, tiled=True).reshape(-1, cell_count)
    got_blocks, got_target = (
        lax.all_to_all(send_blocks, "obs", split_axis=0, concat_axis=0, tiled=True),
        lax.all_to_all(send_target, "obs", split_axis=0, concat_axis=0, tiled=True),
    )
    selected = everything[got_target.reshape(-1)].reshape(got_blocks.shape)
    returned = lax.all_to_all(
        jnp.einsum("pkc,pkc->pk", got_blocks, selected, preferred_element_type=jnp.float32),
        "obs",
        split_axis=0,
        concat_axis=0,
        tiled=True,
    )
    entry_dots = returned.reshape(-1)[slot_index]
    modeled = jnp.sum(jnp.where(sounding_hot, entry_dots[:, None], 0.0), axis=0)
    residual = obs_weight[0] * (modeled - observed[0])
    entry_resid = jnp.sum(jnp.where(sounding_hot, residual[None, :], 0.0), axis=1)
    slot_resid = jnp.zeros((peer_count * slot_cap,), jnp.float32).at[slot_index].set(entry_resid)
    got_resid = lax.all_to_all(
        slot_resid.reshape(peer_count, slot_cap), "obs", split_axis=0, concat_axis=0, tiled=True
    )
    contribution = (got_resid[:, :, None] * got_blocks).astype(jnp.bfloat16)
    targets = got_target
    contribution = contribution.reshape(-1, cell_count)
    targets = targets.reshape(-1)
    row_count = flux.shape[0] * lax.axis_size("tm")
    row_ids = jnp.arange(row_count * tile_dev, dtype=jnp.int32)
    row_match = (row_ids[:, None] == targets[None, :]).astype(jnp.bfloat16)
    summed = jnp.dot(row_match, contribution, preferred_element_type=jnp.float32)
    gradient = lax.psum_scatter(
        summed.reshape(row_count, tile_dev * cell_count), "tm", scatter_dimension=0, tiled=True
    )
    gradient = gradient.reshape(flux.shape[0], tile_dev, cell_count)
    return (modeled[None, :], gradient)


CHUNKS = 8


def eye(n):
    return lax.broadcasted_iota(jnp.int32, (n, n), 0) == lax.broadcasted_iota(jnp.int32, (n, n), 1)


def to_col(row):
    return jnp.sum(jnp.where(eye(row.shape[1]), row, 0.0), axis=1, keepdims=True)


def to_row(col):
    return jnp.sum(jnp.where(eye(col.shape[0]), col, 0.0), axis=0, keepdims=True)


def plane_kernel(
    depth, windows, tile_dev, flux, foot, owner, tile, lag, sounding, swin, observed, weight,
    modeled_out, out,
    staged, gath, foot_all, meta_all, val_all, pick, contrib, part, send_up, send_dn, recv_up, recv_dn, total,
    flux_s, flux_r, meta_s, meta_r, foot_s, foot_r, zup_s, zup_r, zdn_s, zdn_r, val_s, val_r,
    gup_s, gup_r, gdn_s, gdn_r, out_s, out_r, local_sem,
):
    entries, all_cells = foot.shape
    cells = all_cells // 8
    rows_dev = windows * tile_dev
    rows_plane = 8 * rows_dev
    rows_all = depth * rows_plane
    sounds = observed.shape[1]
    pair = 2 * entries
    chunk = cells // CHUNKS
    y = lax.axis_index("tm")
    o = lax.axis_index("obs")
    core = lax.rem(o, 2)
    x = lax.rem(o // 2, 2)
    z = o // 4
    chip = y * 2 + x
    me = chip * 2 + core
    has_up = z < depth - 1
    has_down = z > 0
    above = (y, o + 4)
    below = (y, o - 4)

    def peer(k):
        yy = 1 - y if k & 4 else y
        xx = 1 - x if k & 2 else x
        cc = 1 - core if k & 1 else core
        return yy, xx, cc

    def device(k):
        yy, xx, cc = peer(k)
        return (yy, z * 4 + xx * 2 + cc)

    def place_of(k):
        yy, xx, cc = peer(k)
        return (yy * 2 + xx) * 2 + cc

    def chip_of(q):
        yy, xx, _ = peer(2 * q)
        return yy * 2 + xx

    def eighth(k):
        return pl.ds(pl.multiple_of(place_of(k) * cells, cells), cells)

    def remote(src, dst, send, recv, to):
        return pltpu.make_async_remote_copy(
            src_ref=src, dst_ref=dst, send_sem=send, recv_sem=recv,
            device_id=to, device_id_type=pl.DeviceIdType.MESH,
        )

    barrier = pltpu.get_barrier_semaphore()

    def greet(to):
        pl.semaphore_signal(barrier, inc=1, device_id=to, device_id_type=pl.DeviceIdType.MESH)

    for k in range(1, 8):
        greet(device(k))
    pl.when(has_up)(lambda: greet(above))
    pl.when(has_down)(lambda: greet(below))
    own_flux = pltpu.make_async_copy(flux.at[:, :, eighth(0)], staged.at[z, chip, core], local_sem.at[0])
    own_foot = pltpu.make_async_copy(
        foot.at[:, eighth(0)], foot_all.at[pl.ds(pl.multiple_of(me * entries, entries), entries)], local_sem.at[1]
    )
    own_flux.start()
    own_foot.start()

    hot = lax.broadcasted_iota(jnp.int32, (sounds, entries), 0) == sounding[...]
    window = jnp.sum(
        jnp.where(hot, to_col(swin[...].astype(jnp.float32)), 0.0), axis=0, keepdims=True
    ).astype(jnp.int32) - lag[...]
    own = owner[...]
    late = jnp.where(window >= windows, 1, 0)
    holder = ((own >> 2) * 4 + late * 2 + ((own >> 1) & 1)) * 2 + (own & 1)
    ids = holder * rows_dev + (window - late * windows) * tile_dev + tile[...]
    base = jnp.zeros((1, entries), jnp.float32)
    fill = jnp.zeros((1, pair - sounds), jnp.float32)
    meta_all[me] = jnp.concatenate(
        [
            jnp.concatenate([ids.astype(jnp.float32), base], axis=1),
            jnp.concatenate([(sounding[...] + core * sounds).astype(jnp.float32), base], axis=1),
            jnp.concatenate([observed[...], fill], axis=1),
            jnp.concatenate([weight[...], fill], axis=1),
            jnp.zeros((4, pair), jnp.float32),
        ],
        axis=0,
    )
    pl.semaphore_wait(barrier, 7 + jnp.where(has_up, 1, 0) + jnp.where(has_down, 1, 0))

    def flux_copy(k):
        return remote(
            flux.at[:, :, eighth(k)], staged.at[z, chip, core], flux_s.at[k], flux_r.at[k], device(k)
        )

    def meta_copy(k):
        return remote(meta_all.at[me], meta_all.at[me], meta_s.at[k], meta_r.at[k], device(k))

    def foot_copy(k):
        into = foot_all.at[pl.ds(pl.multiple_of(me * entries, entries), entries)]
        return remote(foot.at[:, eighth(k)], into, foot_s.at[k], foot_r.at[k], device(k))

    def val_copy(k):
        return remote(val_all.at[me], val_all.at[me], val_s.at[k], val_r.at[k], device(k))

    def z_up(zz, q):
        block = staged.at[zz, chip_of(q)]
        return remote(block, block, zup_s.at[zz, q], zup_r.at[zz, q], above)

    def z_dn(zz, q):
        block = staged.at[zz, chip_of(q)]
        return remote(block, block, zdn_s.at[zz, q], zdn_r.at[zz, q], below)

    for k in range(1, 8):
        flux_copy(k).start()
    for k in (6, 7, 2, 4, 3, 5, 1):
        if k == 6:
            for j in range(1, 8):
                meta_copy(j).start()
        foot_copy(k).start()

    def settle(zz, q):
        at = chip_of(q)
        rows = pl.ds(pl.multiple_of(zz * rows_plane + at * 2 * rows_dev, 2 * rows_dev), 2 * rows_dev)

        def body(step, carry):
            span = pl.ds(pl.multiple_of(step * 512, 512), 512)
            gath[rows, span] = staged[zz, at, :, :, :, span].reshape(2 * rows_dev, 512)
            return carry

        lax.fori_loop(0, cells // 512, body, 0)

    for q in range(4):
        if q == 0:
            own_flux.wait()
        else:
            flux_copy(2 * q).wait_recv()
        flux_copy(2 * q + 1).wait_recv()
        pl.when(has_up)(lambda: z_up(z, q).start())
        pl.when(has_down)(lambda: z_dn(z, q).start())
        settle(z, q)
    for s in range(1, depth):
        for q in range(4):
            @pl.when(z >= s)
            def _():
                z_up(z - s, q).wait_recv()
                pl.when(has_up)(lambda: z_up(z - s, q).start())
                settle(z - s, q)

            @pl.when(z + s < depth)
            def _():
                z_dn(z + s, q).wait_recv()
                pl.when(has_down)(lambda: z_dn(z + s, q).start())
                settle(z + s, q)

    for k in range(1, 8):
        meta_copy(k).wait_recv()
    id_rows, hots, obs_cols, wgt_cols = [], [], [], []
    for q in range(4):
        first, second = meta_all[2 * q], meta_all[2 * q + 1]
        both = [jnp.concatenate([first[r : r + 1, :entries], second[r : r + 1, :entries]], axis=1) for r in (0, 1)]
        id_rows.append(both[0].astype(jnp.int32))
        hots.append(
            lax.broadcasted_iota(jnp.int32, (2 * sounds, pair), 0) == both[1].astype(jnp.int32)
        )
        obs_cols.append(
            to_col(jnp.concatenate([first[2:3, :sounds], second[2:3, :sounds]], axis=1))
        )
        wgt_cols.append(
            to_col(jnp.concatenate([first[3:4, :sounds], second[3:4, :sounds]], axis=1))
        )
        row_at = lax.broadcasted_iota(jnp.int32, (rows_all, pair), 0)
        pick[:, q * pair : (q + 1) * pair] = jnp.where(row_at == id_rows[q], 1.0, 0.0).astype(jnp.bfloat16)

    def partial_values(q):
        at = chip_of(q)
        rows = pl.ds(pl.multiple_of(at * pair, pair), pair)
        acc = lax.dot_general(
            gath[...], foot_all[rows, :], (((1,), (1,)), ((), ())), preferred_element_type=jnp.float32
        )
        first, second = meta_all[2 * at], meta_all[2 * at + 1]
        mine = jnp.concatenate([first[0:1, :entries], second[0:1, :entries]], axis=1).astype(jnp.int32)
        row_at = lax.broadcasted_iota(jnp.int32, (rows_all, pair), 0)
        val_all[me, at] = jnp.sum(jnp.where(row_at == mine, acc, 0.0), axis=0, keepdims=True)

    for q in (3, 0, 1, 2):
        if q == 0:
            own_foot.wait()
        else:
            foot_copy(2 * q).wait_recv()
        foot_copy(2 * q + 1).wait_recv()
        partial_values(q)
    for k in (6, 7, 2, 4, 3, 5, 1):
        val_copy(k).start()
    for k in (1, 2, 3, 4, 5, 6, 7):
        val_copy(k).wait_recv()
    model_cols, resids = [], []
    for q in range(4):
        value = val_all[0, q]
        for p in range(1, 8):
            value = value + val_all[p, q]
        model_cols.append(jnp.sum(jnp.where(hots[q], value, 0.0), axis=1, keepdims=True))
        residual = wgt_cols[q] * (model_cols[q] - obs_cols[q])
        resids.append(to_col(jnp.sum(jnp.where(hots[q], residual, 0.0), axis=0, keepdims=True)))

    def span_of(c):
        return pl.ds(pl.multiple_of(c * chunk, chunk), chunk)

    def g_up(d, c):
        span = span_of(c)
        return remote(
            send_up.at[d, :, span], recv_up.at[d, :, span], gup_s.at[d, c], gup_r.at[d, c], above
        )

    def g_dn(d, c):
        span = span_of(c)
        return remote(
            send_dn.at[d, :, span], recv_dn.at[d, :, span], gdn_s.at[d, c], gdn_r.at[d, c], below
        )

    def first(c, carry):
        span = span_of(c)
        for q in range(4):
            rows = pl.ds(q * pair, pair)
            contrib[rows, :] = (resids[q] * foot_all[rows, span].astype(jnp.float32)).astype(jnp.bfloat16)
        summed = jnp.dot(pick[...], contrib[...], preferred_element_type=jnp.float32)
        for d in range(depth):
            part[d, :, span] = summed[d * rows_plane : (d + 1) * rows_plane]

        @pl.when(z == 0)
        def _():
            send_up[depth - 1, :, span] = part[depth - 1, :, span].astype(jnp.bfloat16)
            g_up(depth - 1, c).start()

        @pl.when(z == depth - 1)
        def _():
            send_dn[0, :, span] = part[0, :, span].astype(jnp.bfloat16)
            g_dn(0, c).start()

        return carry

    lax.fori_loop(0, CHUNKS, first, 0)

    for s in range(depth - 2, 0, -1):

        def pass_on(c, carry):
            span = span_of(c)

            @pl.when(z + s < depth)
            def _():
                d = z + s

                @pl.when(z > 0)
                def _():
                    g_up(d, c).wait_recv()
                    summed = part[d, :, span] + recv_up[d, :, span].astype(jnp.float32)
                    send_up[d, :, span] = summed.astype(jnp.bfloat16)

                @pl.when(z == 0)
                def _():
                    send_up[d, :, span] = part[d, :, span].astype(jnp.bfloat16)

                g_up(d, c).start()

            @pl.when(z >= s)
            def _():
                d = z - s

                @pl.when(has_up)
                def _():
                    g_dn(d, c).wait_recv()
                    summed = part[d, :, span] + recv_dn[d, :, span].astype(jnp.float32)
                    send_dn[d, :, span] = summed.astype(jnp.bfloat16)

                @pl.when(z == depth - 1)
                def _():
                    send_dn[d, :, span] = part[d, :, span].astype(jnp.bfloat16)

                g_dn(d, c).start()

            return carry

        lax.fori_loop(0, CHUNKS, pass_on, 0)

    def out_copy(k, c):
        rows = pl.ds(pl.multiple_of(place_of(k) * rows_dev, rows_dev), rows_dev)
        into = pl.ds(pl.multiple_of(me * cells + c * chunk, chunk), chunk)
        return remote(
            total.at[rows, span_of(c)], out.at[:, into], out_s.at[k, c], out_r.at[k, c], device(k)
        )

    def finish(c, carry):
        span = span_of(c)
        total[:, span] = part[z, :, span]

        @pl.when(has_down)
        def _():
            g_up(z, c).wait_recv()
            total[:, span] = total[:, span] + recv_up[z, :, span].astype(jnp.float32)

        @pl.when(has_up)
        def _():
            g_dn(z, c).wait_recv()
            total[:, span] = total[:, span] + recv_dn[z, :, span].astype(jnp.float32)

        for k in (6, 7, 2, 4, 3, 5, 1):
            out_copy(k, c).start()
        into = pl.ds(pl.multiple_of(me * cells + c * chunk, chunk), chunk)
        out[:, into] = total[pl.ds(pl.multiple_of(me * rows_dev, rows_dev), rows_dev), span]
        return carry

    lax.fori_loop(0, CHUNKS, finish, 0)

    modeled = jnp.zeros((1, 2 * sounds), jnp.float32)
    for q in range(4):
        modeled = modeled + jnp.where(chip == q, to_row(model_cols[q]), 0.0)
    modeled_out[...] = jnp.where(core == 0, modeled[:, :sounds], modeled[:, sounds:])

    for k in range(1, 8):
        flux_copy(k).wait_send()
        meta_copy(k).wait_send()
        foot_copy(k).wait_send()
        val_copy(k).wait_send()
    for zz in range(depth):
        for q in range(4):
            pl.when(has_up & (zz <= z))(lambda: z_up(zz, q).wait_send())
            pl.when(has_down & (zz >= z))(lambda: z_dn(zz, q).wait_send())

    def drain(c, carry):
        for d in range(depth):
            pl.when(d > z)(lambda: g_up(d, c).wait_send())
            pl.when(d < z)(lambda: g_dn(d, c).wait_send())
        for k in range(1, 8):
            out_copy(k, c).wait()
        return carry

    lax.fori_loop(0, CHUNKS, drain, 0)


def per_plane(depth, flux, footprint, owner, tile, lag, sounding, swin, observed, weight):
    windows, tile_dev, all_cells = flux.shape
    entries = footprint.shape[0]
    cells = all_cells // 8
    rows_dev = windows * tile_dev
    rows_plane = 8 * rows_dev
    rows_all = depth * rows_plane
    sounds = observed.shape[1]
    bf, f32 = jnp.bfloat16, jnp.float32
    vmem, hbm = pl.BlockSpec(memory_space=pltpu.VMEM), pl.BlockSpec(memory_space=pl.ANY)
    dma = pltpu.SemaphoreType.DMA
    modeled, gradient = pl.pallas_call(
        functools.partial(plane_kernel, depth, windows, tile_dev),
        out_shape=(
            jax.ShapeDtypeStruct((1, sounds), f32),
            jax.ShapeDtypeStruct((rows_dev, all_cells), f32),
        ),
        in_specs=[hbm, hbm] + [vmem] * 7,
        out_specs=(vmem, vmem),
        scratch_shapes=[
            pltpu.VMEM((depth, 4, 2, windows, tile_dev, cells), bf),
            pltpu.VMEM((rows_all, cells), bf),
            pltpu.VMEM((8 * entries, cells), bf),
            pltpu.VMEM((8, 8, 2 * entries), f32),
            pltpu.VMEM((8, 4, 1, 2 * entries), f32),
            pltpu.VMEM((rows_all, 8 * entries), bf),
            pltpu.VMEM((8 * entries, cells // CHUNKS), bf),
            pltpu.VMEM((depth, rows_plane, cells), f32),
            *[pltpu.VMEM((depth, rows_plane, cells), bf)] * 4,
            pltpu.VMEM((rows_plane, cells), f32),
            *[dma((8,))] * 6,
            *[dma((depth, 4))] * 4,
            *[dma((8,))] * 2,
            *[dma((depth, CHUNKS))] * 4,
            *[dma((8, CHUNKS))] * 2,
            dma((2,)),
        ],
        compiler_params=pltpu.CompilerParams(collective_id=0, has_side_effects=True),
    )(flux, footprint, owner.reshape(1, entries), tile, lag, sounding, swin, observed, weight)
    return modeled, gradient.reshape(windows, tile_dev, all_cells)


def solution(mesh):
    placed = (
        P("tm", "obs", None),
        P(("tm", "obs"), None),
        P(("tm", "obs"), None),
        P(("tm", "obs"), None),
        P(("tm", "obs"), None),
        P(("tm", "obs"), None),
        P(("tm", "obs"), None),
        P(("tm", "obs"), None),
        P(("tm", "obs"), None),
    )
    times, places = mesh.shape["tm"], mesh.shape["obs"]
    depth = places // 4
    grouped = times == 2 and places % 4 == 0 and depth >= 2

    def routed(flux, *rest):
        rows = flux.shape[0] * flux.shape[1] * times * places
        fits = rows * flux.shape[2] * 5 <= 40 * 2**20
        plain = flux.shape[0] * flux.shape[1] % 8 == 0 and flux.shape[2] % 16384 == 0
        plain = plain and rest[0].shape[0] % 64 == 0
        body = functools.partial(per_plane, depth) if grouped and fits and plain else per_device
        return body(flux, *rest)

    return jax.shard_map(
        routed,
        mesh=mesh,
        in_specs=placed,
        out_specs=(P(("tm", "obs"), None), P("tm", "obs", None)),
        check_vma=False,
    )
```

time: 98.1 us -> 66.1 us (0.67)
  Pallas kernels: 94.2 us -> 61.8 us
    pallas_call x1, Pallas kernels: 94.2 us -> 61.8 us  [per_plane(): pl.pallas_call(functools.partial(plane_kernel, depth, windows, tile_dev),...]
where the time goes in v1:
time: 66.1 us; the launch traced here: 65.5 us
  Pallas kernels  61.8 us (93%)
  local copies, waits for them, and re-layouts  3.09 us (5%)
    pallas_call x1, Pallas kernels, per_plane(): pl.pallas_call(functools.partial(plane_kernel, depth, windows, tile_dev),...  61.8 us
    reshape x1, local copies, waits for them, and re-layouts, per_plane(): return (modeled, gradient.reshape(windows, tile_dev, all_cells))  1.98 us

profile of v1, /device:TPU:0, one launch (start us, length us, event | category | flops | bytes accessed | tf_op | source)
XLA Modules:
  0.0 65.5 jit_solution(17215890632312918208)
XLA Ops:
  0.6 61.8 %shard_map.104 = (f32[1,16]{1,0:T(1,128)}, f32[8,16384]{1,0:T(8,128)}) custom-call(bf16[2,4,16384]{2,1,0:T(4,128)(2,1)} %flux.1, bf16[64,16384]{1,0:T(8,128)(2,1)} %foot.1, s32[1,64]{1,0:T(1,128)} %bitcast.1, s32[1,64]{1,0:T(1,128)} %tile.1, s32[1,64]{1,0:T(1,128)} %lag.1, s32[1,64]{1,0:T(1,128)} %sounding.1, s32[1,16]{1,0:T(1,128)} %swin.1, ...), custom_call_target="tpu_custom_call" | custom-call | tf_op jit(solution)/shard_map/pallas_call | solution.py:447
  62.4 2.0 %reshape.11 = f32[2,4,16384]{2,1,0:T(4,128)} reshape(f32[8,16384]{1,0:T(8,128)} %get-tuple-element.5) | data formatting | bytes 1048576 | tf_op jit(solution)/shard_map/reshape | solution.py:475
  64.4 1.1 %copy.12 = f32[1,16]{1,0:T(1,128)} copy(f32[1,16]{1,0:T(1,128)} %get-tuple-element.8) | data formatting | bytes 128

commit v2 on v1

--- a/solution.py
+++ b/solution.py
@@ -78,6 +78,7 @@
 
 
 CHUNKS = 8
+FOOT_ORDER = ((1, None), (6, None), (7, None), (2, None), (4, None), (3, 0), (5, 0), (3, 1), (5, 1))
 
 
 def eye(n):
@@ -93,8 +94,8 @@
 
 
 def plane_kernel(
-    depth, windows, tile_dev, flux, foot, owner, tile, lag, sounding, swin, observed, weight,
-    modeled_out, out,
+    depth, windows, tile_dev, flux, foot, owner_h, tile_h, lag_h, sounding_h, swin_h, observed_h, weight_h,
+    modeled_out, out, owner, tile, lag, sounding, swin, observed, weight,
     staged, gath, foot_all, meta_all, val_all, pick, contrib, part, send_up, send_dn, recv_up, recv_dn, total,
     flux_s, flux_r, meta_s, meta_r, foot_s, foot_r, zup_s, zup_r, zdn_s, zdn_r, val_s, val_r,
     gup_s, gup_r, gdn_s, gdn_r, out_s, out_r, local_sem,
@@ -159,9 +160,53 @@
     own_foot = pltpu.make_async_copy(
         foot.at[:, eighth(0)], foot_all.at[pl.ds(pl.multiple_of(me * entries, entries), entries)], local_sem.at[1]
     )
+    pairs = (
+        (owner_h, owner), (tile_h, tile), (lag_h, lag), (sounding_h, sounding),
+        (swin_h, swin), (observed_h, observed), (weight_h, weight),
+    )
+    small = [
+        pltpu.make_async_copy(src, dst, local_sem.at[2 + at]) for at, (src, dst) in enumerate(pairs)
+    ]
+    for copy in small:
+        copy.start()
     own_flux.start()
     own_foot.start()
 
+    pl.semaphore_wait(barrier, 7 + jnp.where(has_up, 1, 0) + jnp.where(has_down, 1, 0))
+
+    def flux_copy(k):
+        return remote(
+            flux.at[:, :, eighth(k)], staged.at[z, chip, core], flux_s.at[k], flux_r.at[k], device(k)
+        )
+
+    def meta_copy(k):
+        return remote(meta_all.at[me], meta_all.at[me], meta_s.at[k], meta_r.at[k], device(k))
+
+    def foot_copy(k, half):
+        rows = pl.ds(pl.multiple_of(me * entries, entries), entries)
+        if half is None:
+            return remote(foot.at[:, eighth(k)], foot_all.at[rows], foot_s.at[0, k], foot_r.at[0, k], device(k))
+        src = pl.ds(pl.multiple_of(place_of(k) * cells + half * (cells // 2), cells // 2), cells // 2)
+        return remote(
+            foot.at[:, src], foot_all.at[rows, pl.ds(half * (cells // 2), cells // 2)],
+            foot_s.at[half, k], foot_r.at[half, k], device(k),
+        )
+
+    def val_copy(k):
+        return remote(val_all.at[me], val_all.at[me], val_s.at[k], val_r.at[k], device(k))
+
+    def z_up(zz, q):
+        block = staged.at[zz, chip_of(q)]
+        return remote(block, block, zup_s.at[zz, q], zup_r.at[zz, q], above)
+
+    def z_dn(zz, q):
+        block = staged.at[zz, chip_of(q)]
+        return remote(block, block, zdn_s.at[zz, q], zdn_r.at[zz, q], below)
+
+    for k in range(1, 8):
+        flux_copy(k).start()
+    for copy in small:
+        copy.wait()
     hot = lax.broadcasted_iota(jnp.int32, (sounds, entries), 0) == sounding[...]
     window = jnp.sum(
         jnp.where(hot, to_col(swin[...].astype(jnp.float32)), 0.0), axis=0, keepdims=True
@@ -182,38 +227,10 @@
         ],
         axis=0,
     )
-    pl.semaphore_wait(barrier, 7 + jnp.where(has_up, 1, 0) + jnp.where(has_down, 1, 0))
-
-    def flux_copy(k):
-        return remote(
-            flux.at[:, :, eighth(k)], staged.at[z, chip, core], flux_s.at[k], flux_r.at[k], device(k)
-        )
-
-    def meta_copy(k):
-        return remote(meta_all.at[me], meta_all.at[me], meta_s.at[k], meta_r.at[k], device(k))
-
-    def foot_copy(k):
-        into = foot_all.at[pl.ds(pl.multiple_of(me * entries, entries), entries)]
-        return remote(foot.at[:, eighth(k)], into, foot_s.at[k], foot_r.at[k], device(k))
-
-    def val_copy(k):
-        return remote(val_all.at[me], val_all.at[me], val_s.at[k], val_r.at[k], device(k))
-
-    def z_up(zz, q):
-        block = staged.at[zz, chip_of(q)]
-        return remote(block, block, zup_s.at[zz, q], zup_r.at[zz, q], above)
-
-    def z_dn(zz, q):
-        block = staged.at[zz, chip_of(q)]
-        return remote(block, block, zdn_s.at[zz, q], zdn_r.at[zz, q], below)
-
     for k in range(1, 8):
-        flux_copy(k).start()
-    for k in (6, 7, 2, 4, 3, 5, 1):
-        if k == 6:
-            for j in range(1, 8):
-                meta_copy(j).start()
-        foot_copy(k).start()
+        meta_copy(k).start()
+    for k, half in FOOT_ORDER:
+        foot_copy(k, half).start()
 
     def settle(zz, q):
         at = chip_of(q)
@@ -268,33 +285,54 @@
         row_at = lax.broadcasted_iota(jnp.int32, (rows_all, pair), 0)
         pick[:, q * pair : (q + 1) * pair] = jnp.where(row_at == id_rows[q], 1.0, 0.0).astype(jnp.bfloat16)
 
-    def partial_values(q):
-        at = chip_of(q)
-        rows = pl.ds(pl.multiple_of(at * pair, pair), pair)
+    def ids_of(k):
+        return meta_all[place_of(k)][0:1, :entries]
+
+    def rows_of(k):
+        return pl.ds(pl.multiple_of(place_of(k) * entries, entries), entries)
+
+    def partial_values(a, b, span):
         acc = lax.dot_general(
-            gath[...], foot_all[rows, :], (((1,), (1,)), ((), ())), preferred_element_type=jnp.float32
-        )
-        first, second = meta_all[2 * at], meta_all[2 * at + 1]
-        mine = jnp.concatenate([first[0:1, :entries], second[0:1, :entries]], axis=1).astype(jnp.int32)
+            gath[:, span],
+            jnp.concatenate([foot_all[rows_of(a), span], foot_all[rows_of(b), span]], axis=0),
+            (((1,), (1,)), ((), ())),
+            preferred_element_type=jnp.float32,
+        )
+        wanted = jnp.concatenate([ids_of(a), ids_of(b)], axis=1).astype(jnp.int32)
         row_at = lax.broadcasted_iota(jnp.int32, (rows_all, pair), 0)
-        val_all[me, at] = jnp.sum(jnp.where(row_at == mine, acc, 0.0), axis=0, keepdims=True)
-
-    for q in (3, 0, 1, 2):
-        if q == 0:
-            own_foot.wait()
-        else:
-            foot_copy(2 * q).wait_recv()
-        foot_copy(2 * q + 1).wait_recv()
-        partial_values(q)
+        return jnp.sum(jnp.where(row_at == wanted, acc, 0.0), axis=0, keepdims=True)
+
+    def keep_values(a, b, found):
+        val_all[me, place_of(a)] = found[:, :entries]
+        val_all[me, place_of(b)] = found[:, entries:]
+
+    whole = pl.ds(0, cells)
+    for a, b in ((0, 1), (6, 7), (2, 4)):
+        for k in (a, b):
+            if k:
+                foot_copy(k, None).wait_recv()
+            else:
+                own_foot.wait()
+        keep_values(a, b, partial_values(a, b, whole))
+    last = jnp.zeros((1, pair), jnp.float32)
+    for half in range(2):
+        foot_copy(3, half).wait_recv()
+        foot_copy(5, half).wait_recv()
+        last = last + partial_values(3, 5, pl.ds(half * (cells // 2), cells // 2))
+    keep_values(3, 5, last)
     for k in (6, 7, 2, 4, 3, 5, 1):
         val_copy(k).start()
     for k in (1, 2, 3, 4, 5, 6, 7):
         val_copy(k).wait_recv()
     model_cols, resids = [], []
     for q in range(4):
-        value = val_all[0, q]
-        for p in range(1, 8):
-            value = value + val_all[p, q]
+        sums = []
+        for b in (2 * q, 2 * q + 1):
+            value = val_all[0, b]
+            for p in range(1, 8):
+                value = value + val_all[p, b]
+            sums.append(value)
+        value = jnp.concatenate(sums, axis=1)
         model_cols.append(jnp.sum(jnp.where(hots[q], value, 0.0), axis=1, keepdims=True))
         residual = wgt_cols[q] * (model_cols[q] - obs_cols[q])
         resids.append(to_col(jnp.sum(jnp.where(hots[q], residual, 0.0), axis=0, keepdims=True)))
@@ -415,8 +453,9 @@
     for k in range(1, 8):
         flux_copy(k).wait_send()
         meta_copy(k).wait_send()
-        foot_copy(k).wait_send()
         val_copy(k).wait_send()
+    for k, half in FOOT_ORDER:
+        foot_copy(k, half).wait_send()
     for zz in range(depth):
         for q in range(4):
             pl.when(has_up & (zz <= z))(lambda: z_up(zz, q).wait_send())
@@ -431,6 +470,11 @@
         return carry
 
     lax.fori_loop(0, CHUNKS, drain, 0)
+
+
+def deliver(modeled, gradient, modeled_out, gradient_out):
+    modeled_out[...] = modeled[...]
+    gradient_out[...] = gradient[...].reshape(gradient_out.shape)
 
 
 def per_plane(depth, flux, footprint, owner, tile, lag, sounding, swin, observed, weight):
@@ -450,29 +494,41 @@
             jax.ShapeDtypeStruct((1, sounds), f32),
             jax.ShapeDtypeStruct((rows_dev, all_cells), f32),
         ),
-        in_specs=[hbm, hbm] + [vmem] * 7,
+        in_specs=[hbm] * 9,
         out_specs=(vmem, vmem),
         scratch_shapes=[
+            *[pltpu.VMEM((1, entries), jnp.int32)] * 4,
+            pltpu.VMEM((1, sounds), jnp.int32),
+            *[pltpu.VMEM((1, sounds), f32)] * 2,
             pltpu.VMEM((depth, 4, 2, windows, tile_dev, cells), bf),
             pltpu.VMEM((rows_all, cells), bf),
             pltpu.VMEM((8 * entries, cells), bf),
             pltpu.VMEM((8, 8, 2 * entries), f32),
-            pltpu.VMEM((8, 4, 1, 2 * entries), f32),
+            pltpu.VMEM((8, 8, 1, entries), f32),
             pltpu.VMEM((rows_all, 8 * entries), bf),
             pltpu.VMEM((8 * entries, cells // CHUNKS), bf),
             pltpu.VMEM((depth, rows_plane, cells), f32),
             *[pltpu.VMEM((depth, rows_plane, cells), bf)] * 4,
             pltpu.VMEM((rows_plane, cells), f32),
-            *[dma((8,))] * 6,
+            *[dma((8,))] * 4,
+            *[dma((2, 8))] * 2,
             *[dma((depth, 4))] * 4,
             *[dma((8,))] * 2,
             *[dma((depth, CHUNKS))] * 4,
             *[dma((8, CHUNKS))] * 2,
-            dma((2,)),
+            dma((9,)),
         ],
         compiler_params=pltpu.CompilerParams(collective_id=0, has_side_effects=True),
     )(flux, footprint, owner.reshape(1, entries), tile, lag, sounding, swin, observed, weight)
-    return modeled, gradient.reshape(windows, tile_dev, all_cells)
+    return pl.pallas_call(
+        deliver,
+        out_shape=(
+            jax.ShapeDtypeStruct((1, sounds), f32),
+            jax.ShapeDtypeStruct((windows, tile_dev, all_cells), f32),
+        ),
+        in_specs=[vmem] * 2,
+        out_specs=(vmem, vmem),
+    )(modeled, gradient)
 
 
 def solution(mesh):

time: 66.1 us -> 64.5 us (0.976)
  local copies, waits for them, and re-layouts: 3.09 us -> 0 us
  Pallas kernels: 61.8 us -> 63.7 us
    reshape x1 -> x0, local copies, waits for them, and re-layouts: 1.98 us -> none  [per_plane(): return (modeled, gradient.reshape(windows, tile_dev, all_cells))]
    pallas_call x0 -> x1, Pallas kernels: none -> 1.88 us  [per_plane(): pl.pallas_call(deliver, out_shape=(jax.ShapeDtypeStruct((1, sounds), f32)...]
    unnamed x1 -> x0, local copies, waits for them, and re-layouts: 1.11 us -> none
where the time goes in v2:
time: 64.5 us; the launch traced here: 64.3 us
  Pallas kernels  63.7 us (99%)
    pallas_call x1, Pallas kernels, per_plane(): pl.pallas_call(functools.partial(plane_kernel, depth, windows, tile_dev),...  61.8 us
    pallas_call x1, Pallas kernels, per_plane(): pl.pallas_call(deliver, out_shape=(jax.ShapeDtypeStruct((1, sounds), f32)...  1.88 us

profile of v2, /device:TPU:0, one launch (start us, length us, event | category | flops | bytes accessed | tf_op | source)
XLA Modules:
  0.0 64.3 jit_solution(15282682235102792945)
XLA Ops:
  0.6 61.8 %shard_map.104 = (f32[1,16]{1,0:T(1,128)}, f32[8,16384]{1,0:T(8,128)}) custom-call(bf16[2,4,16384]{2,1,0:T(4,128)(2,1)} %flux.1, bf16[64,16384]{1,0:T(8,128)(2,1)} %foot.1, s32[1,64]{1,0:T(1,128)} %bitcast.1, s32[1,64]{1,0:T(1,128)} %tile_h.1, s32[1,64]{1,0:T(1,128)} %lag_h.1, s32[1,64]{1,0:T(1,128)} %sounding_h.1, s32[1,16]{1,0:T(1,128)} %swin_h.1, ...), custom_call_target="tpu_custom_call" | custom-call | tf_op jit(solution)/shard_map/pallas_call | solution.py:491
  62.5 1.9 %shard_map.105 = (f32[1,16]{1,0:T(1,128)}, f32[2,4,16384]{2,1,0:T(4,128)}) custom-call(f32[1,16]{1,0:T(1,128)} %get-tuple-element.4.modeled, f32[8,16384]{1,0:T(8,128)} %get-tuple-element.5.gradient), custom_call_target="tpu_custom_call" | custom-call | tf_op jit(solution)/shard_map/pallas_call | solution.py:523
